TPU v7x, 256 devices: a whole 4x4x8 slice. The times are simulated.
256 devices in a mesh: dp: 8 (over z), section: 4 (over y_hi, core), seq: 8 (over y_lo, x).
Axes of the slice: x: 4, y: 4 (y_hi: 2, y_lo: 2; y = y_hi * 2 + y_lo), z: 8, core: 2. Of those that a mesh axis runs over, the one named last changes fastest.
Arguments:
- acts: bfloat16 [8, 1024, 1536], P('dp', 'seq'), may hold values from -6 to 6
- cotangent: bfloat16 [8, 1024, 1536], P('dp', 'seq'), may hold values from -6 to 6
- gains: bfloat16 [4, 1536], P('section'), may hold values from 0.5 to 1.5
- w_query: bfloat16 [4, 1536, 256], P('section'), may hold values from -0.15625 to 0.15625
- w_key: bfloat16 [4, 1536, 256], P('section'), may hold values from -0.15625 to 0.15625
- w_value: bfloat16 [4, 1536, 384], P('section'), may hold values from -0.15625 to 0.15625
- w_out: bfloat16 [4, 1536, 384], P('section'), may hold values from -0.3125 to 0.3125
Outputs:
- d_acts: bfloat16 [8, 1024, 1536], P('dp', 'seq', 'section')
- g_gains: float32 [4, 1536], P('section', ('dp', 'seq'))
- g_query: float32 [4, 1536, 256], P('section', ('dp', 'seq'))
- g_key: float32 [4, 1536, 256], P('section', ('dp', 'seq'))
- g_value: float32 [4, 1536, 384], P('section', ('dp', 'seq'))
- g_out: float32 [4, 1536, 384], P('section', ('dp', 'seq'))
All inputs are finite; a program needn't handle non-finite values.
Results may differ from a plain program's by a relative error of at most 0.02.
Values may be sent and summed in bfloat16 or wider, within the bound.
No kernel may reach another device: no remote copies, remote signals or barrier semaphores. Data moves between devices by JAX's collectives and lax.ppermute only.
A program may use at most 64 MiB of HBM per device.

v0:
```python
import jax
import jax.numpy as jnp
from jax import lax
from jax.sharding import PartitionSpec as P

HEADS = 4
KEY = 64
VALUE = 96
epsilon = 1e-05


def passed_along(block, axis, distance):
    devices = range(lax.axis_size(axis))
    route = [(i - distance, i) for i in devices if i - distance in devices]
    return lax.ppermute(block, axis, route)


def from_root(block, axis, owner):
    block = jnp.where(lax.axis_index(axis) == owner, block, jnp.zeros_like(block))
    return lax.psum(block, axis)


def layer_norm(inputs, norm_gain):
    widened = inputs.astype(jnp.float32)
    centred = widened - jnp.mean(widened, axis=-1, keepdims=True)
    inverse = lax.rsqrt(jnp.mean(centred * centred, axis=-1, keepdims=True) + epsilon)
    normed = centred * inverse
    return ((normed * norm_gain.astype(jnp.float32)).astype(jnp.bfloat16), normed, inverse)


def split_heads(matrix, width):
    return matrix.reshape(matrix.shape[0], HEADS, width)


def times_transposed(left, right):
    return jnp.einsum("ic,dc->id", left, right, preferred_element_type=jnp.float32)


def outer_sum(left, right):
    return jnp.einsum("id,ic->dc", left, right, preferred_element_type=jnp.float32)


def exp_scores_of(query_local, key_all):
    score_scale = KEY ** (-0.5)
    raw_scores = jnp.einsum(
        "ihc,jhc->hij",
        split_heads(query_local, KEY),
        split_heads(key_all, KEY),
        preferred_element_type=jnp.float32,
    )
    return jnp.exp(raw_scores * score_scale)


def forward_layer(inputs, weights):
    norm_gain, proj_query, proj_key, proj_value, proj_out = weights
    row_count = inputs.shape[0]
    normal_bf, normed, inverse = layer_norm(inputs, norm_gain)
    query_local = jnp.dot(normal_bf, proj_query, preferred_element_type=jnp.float32).astype(
        jnp.bfloat16
    )
    key_local = jnp.dot(normal_bf, proj_key, preferred_element_type=jnp.float32).astype(
        jnp.bfloat16
    )
    value_local = jnp.dot(normal_bf, proj_value, preferred_element_type=jnp.float32).astype(
        jnp.bfloat16
    )
    key_all, value_all = (
        lax.all_gather(key_local, "seq", axis=0, tiled=True),
        lax.all_gather(value_local, "seq", axis=0, tiled=True),
    )
    expo = exp_scores_of(query_local, key_all)
    totals = jnp.sum(expo, axis=-1)
    rounded = expo.astype(jnp.bfloat16)
    numerator = jnp.einsum(
        "hij,jhc->ihc", rounded, split_heads(value_all, VALUE), preferred_element_type=jnp.float32
    )
    attended = (
        (numerator / totals.T[:, :, None]).astype(jnp.bfloat16).reshape(row_count, HEADS * VALUE)
    )
    mixed_out = inputs.astype(jnp.float32) + times_transposed(attended, proj_out)
    record = (
        normal_bf,
        normed,
        inverse,
        query_local,
        key_local,
        value_local,
        key_all,
        value_all,
        totals,
        attended,
    )
    return (mixed_out.astype(jnp.bfloat16), record)


def backward_layer(grad_in, record, weights):
    norm_gain, proj_query, proj_key, proj_value, proj_out = weights
    (
        normal_bf,
        normed,
        inverse,
        query_local,
        key_local,
        value_local,
        key_all,
        value_all,
        totals,
        attended,
    ) = record
    row_count = grad_in.shape[0]
    score_scale = KEY ** (-0.5)
    grad_out_w = outer_sum(grad_in, attended)
    grad_attended = jnp.dot(grad_in, proj_out, preferred_element_type=jnp.float32).astype(
        jnp.bfloat16
    )
    grad_scaled = (
        split_heads(grad_attended, VALUE).astype(jnp.float32) / totals.T[:, :, None]
    ).astype(jnp.bfloat16)
    correction = jnp.sum(
        grad_scaled.astype(jnp.float32) * split_heads(attended, VALUE).astype(jnp.float32), axis=-1
    ).astype(jnp.bfloat16)
    query_heads = split_heads(query_local, KEY)
    expo = exp_scores_of(query_local, key_all)
    grad_probs = jnp.einsum(
        "ihc,jhc->hij",
        grad_scaled,
        split_heads(value_all, VALUE),
        preferred_element_type=jnp.float32,
    )
    grad_scores = (
        expo * (grad_probs - correction.astype(jnp.float32).T[:, :, None]) * score_scale
    ).astype(jnp.bfloat16)
    grad_query = jnp.einsum(
        "hij,jhc->ihc", grad_scores, split_heads(key_all, KEY), preferred_element_type=jnp.float32
    )
    grad_query = grad_query.astype(jnp.bfloat16).reshape(row_count, HEADS * KEY)
    rounded = expo.astype(jnp.bfloat16)
    part_key = jnp.einsum(
        "hij,ihc->jhc", grad_scores, query_heads, preferred_element_type=jnp.float32
    )
    part_value = jnp.einsum(
        "hij,ihc->jhc", rounded, grad_scaled, preferred_element_type=jnp.float32
    )
    full_rows = part_key.shape[0]
    key_sum, value_sum = (
        lax.psum_scatter(
            part_key.reshape(full_rows, HEADS * KEY).astype(jnp.bfloat16),
            "seq",
            scatter_dimension=0,
            tiled=True,
        ).astype(jnp.float32),
        lax.psum_scatter(
            part_value.reshape(full_rows, HEADS * VALUE).astype(jnp.bfloat16),
            "seq",
            scatter_dimension=0,
            tiled=True,
        ).astype(jnp.float32),
    )
    grad_key = key_sum.astype(jnp.bfloat16)
    grad_value = value_sum.astype(jnp.bfloat16)
    grad_query_w = outer_sum(normal_bf, grad_query)
    grad_key_w = outer_sum(normal_bf, grad_key)
    grad_value_w = outer_sum(normal_bf, grad_value)
    grad_normal = times_transposed(grad_query, proj_query)
    grad_normal = grad_normal + times_transposed(grad_key, proj_key)
    grad_normal = grad_normal + times_transposed(grad_value, proj_value)
    grad_gain = jnp.sum(grad_normal * normed, axis=0)
    grad_normed = grad_normal * norm_gain.astype(jnp.float32)
    grad_inputs = inverse * (
        grad_normed
        - jnp.mean(grad_normed, axis=-1, keepdims=True)
        - normed * jnp.mean(grad_normed * normed, axis=-1, keepdims=True)
    )
    passed = (grad_in.astype(jnp.float32) + grad_inputs).astype(jnp.bfloat16)
    return (passed, (grad_gain, grad_query_w, grad_key_w, grad_value_w, grad_out_w))


def shards(acts, cotangent, gains, w_query, w_key, w_value, w_out):
    weights = (gains[0], w_query[0], w_key[0], w_value[0], w_out[0])
    section_now = lax.axis_index("section")
    section_count = lax.axis_size("section")
    inputs = acts[0]
    saved = None
    for section_step in range(section_count):
        output, record = forward_layer(inputs, weights)
        if section_step == 0:
            saved = record
        else:
            saved = jax.tree.map(
                lambda latest, earlier: jnp.where(section_now == section_step, latest, earlier),
                record,
                saved,
            )
        if section_step + 1 < section_count:
            inputs = passed_along(output, "section", 1)
    grad_flow = cotangent[0]
    grad_terms = None
    passed = grad_flow
    for section_step in reversed(range(section_count)):
        passed, fresh_terms = backward_layer(grad_flow, saved, weights)
        if section_step == section_count - 1:
            grad_terms = fresh_terms
        else:
            grad_terms = jax.tree.map(
                lambda latest, earlier: jnp.where(section_now == section_step, latest, earlier),
                fresh_terms,
                grad_terms,
            )
        if section_step > 0:
            grad_flow = passed_along(passed, "section", -1)
    input_grad = from_root(passed, "section", 0)
    channel_share = input_grad.shape[1] // section_count
    own_channels = lax.dynamic_slice_in_dim(
        input_grad, section_now * channel_share, channel_share, 1
    )
    grad_gain, grad_query_w, grad_key_w, grad_value_w, grad_out_w = grad_terms
    sums = (
        lax.psum_scatter(grad_gain[None], ("dp", "seq"), scatter_dimension=1, tiled=True),
        lax.psum_scatter(grad_query_w[None], ("dp", "seq"), scatter_dimension=1, tiled=True),
        lax.psum_scatter(grad_key_w[None], ("dp", "seq"), scatter_dimension=1, tiled=True),
        lax.psum_scatter(grad_value_w[None], ("dp", "seq"), scatter_dimension=1, tiled=True),
        lax.psum_scatter(grad_out_w[None], ("dp", "seq"), scatter_dimension=1, tiled=True),
    )
    return (own_channels[None], sums[0], sums[1], sums[2], sums[3], sums[4])


def solution(mesh):
    return jax.shard_map(
        shards,
        mesh=mesh,
        in_specs=(
            P("dp", "seq", None),
            P("dp", "seq", None),
            P("section", None),
            P("section", None, None),
            P("section", None, None),
            P("section", None, None),
            P("section", None, None),
        ),
        out_specs=(
            P("dp", "seq", "section"),
            P("section", ("dp", "seq")),
            P("section", ("dp", "seq"), None),
            P("section", ("dp", "seq"), None),
            P("section", ("dp", "seq"), None),
            P("section", ("dp", "seq"), None),
        ),
        check_vma=False,
    )
```

profile of v0, /device:TPU:16, one launch (start us, length us, event | category | flops | bytes accessed | tf_op | source)
XLA Modules:
  0.0 2088.0 jit_solution(8954973873401913931)
XLA Ops:
  13.6 29.1 %all_gather.25 = bf16[1024,256]{1,0:T(8,128)(2,1)S(1)} all-gather(bf16[128,256]{1,0:T(8,128)(2,1)S(1)} %convolution_convert_fusion.14), channel_id=1, replica_groups=mesh['dp'=8,'section'=4,'seq'=8] {'seq'}, dimensions={0}, use_global_device_ids=true | all-gather | bytes 589824 | tf_op jit(solution)/shard_map/all_gather | solution.py:68
  43.6 29.5 %all_gather.24 = bf16[1024,384]{1,0:T(8,128)(2,1)S(1)} all-gather(bf16[128,384]{1,0:T(8,128)(2,1)S(1)} %fusion.52), channel_id=1, replica_groups=mesh['dp'=8,'section'=4,'seq'=8] {'seq'}, dimensions={0}, use_global_device_ids=true | all-gather | bytes 884736 | tf_op jit(solution)/shard_map/all_gather | solution.py:69
  79.7 8.7 collective-permute-done
  93.6 31.0 %all_gather.27 = bf16[1024,256]{1,0:T(8,128)(2,1)} all-gather(bf16[128,256]{1,0:T(8,128)(2,1)S(1)} %convolution_convert_fusion.12), channel_id=1, replica_groups=mesh['dp'=8,'section'=4,'seq'=8] {'seq'}, dimensions={0}, use_global_device_ids=true | all-gather | bytes 589824 | tf_op jit(solution)/shard_map/all_gather | solution.py:68
  127.7 31.3 %all_gather.26 = bf16[1024,384]{1,0:T(8,128)(2,1)} all-gather(bf16[128,384]{1,0:T(8,128)(2,1)S(1)} %fusion.55), channel_id=1, replica_groups=mesh['dp'=8,'section'=4,'seq'=8] {'seq'}, dimensions={0}, use_global_device_ids=true | all-gather | bytes 884736 | tf_op jit(solution)/shard_map/all_gather | solution.py:69
  166.0 9.0 collective-permute-done.1
  180.3 30.8 %all_gather.29 = bf16[1024,256]{1,0:T(8,128)(2,1)} all-gather(bf16[128,256]{1,0:T(8,128)(2,1)S(1)} %convolution_convert_fusion.10), channel_id=1, replica_groups=mesh['dp'=8,'section'=4,'seq'=8] {'seq'}, dimensions={0}, use_global_device_ids=true | all-gather | bytes 589824 | tf_op jit(solution)/shard_map/all_gather | solution.py:68
  214.4 31.3 %all_gather.28 = bf16[1024,384]{1,0:T(8,128)(2,1)} all-gather(bf16[128,384]{1,0:T(8,128)(2,1)S(1)} %fusion.58), channel_id=1, replica_groups=mesh['dp'=8,'section'=4,'seq'=8] {'seq'}, dimensions={0}, use_global_device_ids=true | all-gather | bytes 884736 | tf_op jit(solution)/shard_map/all_gather | solution.py:69
  257.2 5.4 collective-permute-done.2
  265.7 28.9 %all_gather.30 = bf16[1024,256]{1,0:T(8,128)(2,1)S(1)} all-gather(bf16[128,256]{1,0:T(8,128)(2,1)S(1)} %convolution_convert_fusion.9), channel_id=1, replica_groups=mesh['dp'=8,'section'=4,'seq'=8] {'seq'}, dimensions={0}, use_global_device_ids=true | all-gather | bytes 589824 | tf_op jit(solution)/shard_map/all_gather | solution.py:68
  299.6 29.4 %all_gather.31 = bf16[1024,384]{1,0:T(8,128)(2,1)S(1)} all-gather(bf16[128,384]{1,0:T(8,128)(2,1)S(1)} %fusion.61), channel_id=1, replica_groups=mesh['dp'=8,'section'=4,'seq'=8] {'seq'}, dimensions={0}, use_global_device_ids=true | all-gather | bytes 884736 | tf_op jit(solution)/shard_map/all_gather | solution.py:69
  358.2 36.1 %reduce-scatter.42.cloned.1.call-done = bf16[128,256]{1,0:T(8,128)(2,1)} async-done(((bf16[1024,256]{1,0:T(8,128)(2,1)}), bf16[128,256]{1,0:T(8,128)(2,1)}) %reduce-scatter.42.cloned.1.call-update) | async-done | bytes 65552
  396.8 40.3 %reduce-scatter.44.cloned.1.call-done = bf16[128,384]{1,0:T(8,128)(2,1)} async-done(((bf16[1024,384]{1,0:T(8,128)(2,1)}), bf16[128,384]{1,0:T(8,128)(2,1)}) %reduce-scatter.44.cloned.1.call-update) | async-done | bytes 98320
  467.6 31.4 %reduce-scatter.46.cloned.1.call-done = bf16[128,256]{1,0:T(8,128)(2,1)} async-done(((bf16[1024,256]{1,0:T(8,128)(2,1)}), bf16[128,256]{1,0:T(8,128)(2,1)}) %reduce-scatter.46.cloned.1.call-update) | async-done | bytes 65552
  501.7 39.9 %reduce-scatter.48.cloned.1.call-done = bf16[128,384]{1,0:T(8,128)(2,1)} async-done(((bf16[1024,384]{1,0:T(8,128)(2,1)}), bf16[128,384]{1,0:T(8,128)(2,1)}) %reduce-scatter.48.cloned.1.call-update) | async-done | bytes 98320
  571.6 31.2 %reduce-scatter.50.cloned.1.call-done = bf16[128,256]{1,0:T(8,128)(2,1)} async-done(((bf16[1024,256]{1,0:T(8,128)(2,1)}), bf16[128,256]{1,0:T(8,128)(2,1)}) %reduce-scatter.50.cloned.1.call-update) | async-done | bytes 65552
  605.4 40.0 %reduce-scatter.52.cloned.1.call-done = bf16[128,384]{1,0:T(8,128)(2,1)} async-done(((bf16[1024,384]{1,0:T(8,128)(2,1)}), bf16[128,384]{1,0:T(8,128)(2,1)}) %reduce-scatter.52.cloned.1.call-update) | async-done | bytes 98320
  679.0 27.4 %reduce-scatter.54.cloned.1.call-done = bf16[128,256]{1,0:T(8,128)(2,1)} async-done(((bf16[1024,256]{1,0:T(8,128)(2,1)}), bf16[128,256]{1,0:T(8,128)(2,1)}) %reduce-scatter.54.cloned.1.call-update) | async-done | bytes 65552
  708.8 40.3 %reduce-scatter.56.cloned.1.call-done = bf16[128,384]{1,0:T(8,128)(2,1)} async-done(((bf16[1024,384]{1,0:T(8,128)(2,1)}), bf16[128,384]{1,0:T(8,128)(2,1)}) %reduce-scatter.56.cloned.1.call-update) | async-done | bytes 98320
  771.8 157.9 %all-reduce = f32[1,1536]{1,0:T(1,128)S(1)} all-reduce(f32[1,1536]{1,0:T(1,128)S(1)} %select_n.362), channel_id=10, replica_groups=mesh['dp'=8,'section'=4,'seq'=8] {'dp','seq'}, use_global_device_ids=true, to_apply=%region_37.38.clone | all-reduce | flops 1536 | bytes 12288
  931.9 188.5 %reduce-scatter.38.cloned.1.call-done = f32[1,24,256]{2,1,0:T(8,128)} async-done(((f32[1,1536,256]{2,1,0:T(8,128)}), f32[1,24,256]{2,1,0:T(8,128)}) %reduce-scatter.38.cloned.1.call-update) | async-done | bytes 24592 | tf_op jit(solution)/shard_map/reduce_scatter | solution.py:219
  1120.3 318.8 %reduce-scatter.40.cloned.1.call-done = f32[1,24,256]{2,1,0:T(8,128)} async-done(((f32[1,1536,256]{2,1,0:T(8,128)}), f32[1,24,256]{2,1,0:T(8,128)}) %reduce-scatter.40.cloned.1.call-update) | async-done | bytes 24592 | tf_op jit(solution)/shard_map/reduce_scatter | solution.py:220
  1439.1 320.8 %reduce-scatter.60.cloned.1.call-done = f32[1,24,384]{2,1,0:T(8,128)} async-done(((f32[1,1536,384]{2,1,0:T(8,128)}), f32[1,24,384]{2,1,0:T(8,128)}) %reduce-scatter.60.cloned.1.call-update) | async-done | bytes 36880
  1759.9 321.2 %reduce-scatter.58.cloned.1.call-done = f32[1,24,384]{2,1,0:T(8,128)} async-done(((f32[1,1536,384]{2,1,0:T(8,128)}), f32[1,24,384]{2,1,0:T(8,128)}) %reduce-scatter.58.cloned.1.call-update) | async-done | bytes 36880
  (406 shorter events, 213.7 us)
Async XLA Ops:
  7.2 387.1 %reduce-scatter.42.cloned.1.call-start = ((), (), s32[]{:S(2)}) async-start(), calls=%async_computation.15 | async-start | bytes 589824
  77.8 10.6 collective-permute-start
  88.4 75.1 %copy-start.29 = (bf16[128,1536]{1,0:T(8,128)(2,1)}, bf16[128,1536]{1,0:T(8,128)(2,1)S(1)}, u32[]{:S(2)}) copy-start(bf16[128,1536]{1,0:T(8,128)(2,1)S(1)} %collective-permute-done) | copy-start | bytes 1179652
  164.1 11.0 collective-permute-start.1
  175.0 75.2 %copy-start.31 = (bf16[128,1536]{1,0:T(8,128)(2,1)}, bf16[128,1536]{1,0:T(8,128)(2,1)S(1)}, u32[]{:S(2)}) copy-start(bf16[128,1536]{1,0:T(8,128)(2,1)S(1)} %collective-permute-done.1) | copy-start | bytes 1179652
  251.5 11.2 collective-permute-start.2
  262.6 70.7 %copy-start.40 = (bf16[128,1536]{1,0:T(8,128)(2,1)}, bf16[128,1536]{1,0:T(8,128)(2,1)S(1)}, u32[]{:S(2)}) copy-start(bf16[128,1536]{1,0:T(8,128)(2,1)S(1)} %collective-permute-done.2) | copy-start | bytes 1179652
  349.9 87.1 %reduce-scatter.44.cloned.1.call-start = ((), (), s32[]{:S(2)}) async-start(), calls=%async_computation.16 | async-start | bytes 884736
  354.5 144.5 %reduce-scatter.46.cloned.1.call-start = ((), (), s32[]{:S(2)}) async-start(), calls=%async_computation.17 | async-start | bytes 589824
  356.4 80.7 %copy-start.28 = (bf16[1,128,1536]{2,1,0:T(8,128)(2,1)S(1)}, bf16[1,128,1536]{2,1,0:T(8,128)(2,1)}, u32[]{:S(2)}) copy-start(bf16[1,128,1536]{2,1,0:T(8,128)(2,1)} %param.7) | copy-start | bytes 1179652
  396.8 43.4 %copy-start.95 = (f32[128]{0:T(128)S(1)}, f32[128]{0:T(128)}, u32[]{:S(2)}) copy-start(f32[128]{0:T(128)} %get-tuple-element.28) | copy-start | bytes 1540
  440.4 7.2 collective-permute-start.3
  458.8 82.8 %reduce-scatter.48.cloned.1.call-start = ((), (), s32[]{:S(2)}) async-start(), calls=%async_computation.18 | async-start | bytes 884736
  463.7 139.1 %reduce-scatter.50.cloned.1.call-start = ((), (), s32[]{:S(2)}) async-start(), calls=%async_computation.19 | async-start | bytes 589824
  544.3 7.2 collective-permute-start.4
  562.6 82.8 %reduce-scatter.52.cloned.1.call-start = ((), (), s32[]{:S(2)}) async-start(), calls=%async_computation.20 | async-start | bytes 884736
  567.7 138.6 %reduce-scatter.54.cloned.1.call-start = ((), (), s32[]{:S(2)}) async-start(), calls=%async_computation.21 | async-start | bytes 589824
  648.1 7.2 collective-permute-start.5
  666.3 82.9 %reduce-scatter.56.cloned.1.call-start = ((), (), s32[]{:S(2)}) async-start(), calls=%async_computation.22 | async-start | bytes 884736
  670.9 259.4 %all-reduce.5.cloned.1.call-start = ((), (), s32[]{:S(2)}) async-start(), calls=%async_computation.12 | async-start | bytes 786432 | tf_op jit(solution)/shard_map/psum | solution.py:20
  752.1 368.2 %reduce-scatter.38.cloned.1.call-start = ((), (), s32[]{:S(2)}) async-start(), calls=%async_computation.13 | async-start | bytes 1597440 | tf_op jit(solution)/shard_map/reduce_scatter | solution.py:219
  756.5 682.6 %reduce-scatter.40.cloned.1.call-start = ((), (), s32[]{:S(2)}) async-start(), calls=%async_computation.14 | async-start | bytes 1597440 | tf_op jit(solution)/shard_map/reduce_scatter | solution.py:220
  759.8 1000.1 %reduce-scatter.60.cloned.1.call-start = ((), (), s32[]{:S(2)}) async-start(), calls=%async_computation.24 | async-start | bytes 2396160
  764.8 1316.3 %reduce-scatter.58.cloned.1.call-start = ((), (), s32[]{:S(2)}) async-start(), calls=%async_computation.23 | async-start | bytes 2396160
  (108 other events, 732.3 us)
Sparse Core Ops, SparseCore 0:
  350.0 44.2 reduce-scatter.41
  396.9 40.1 reduce-scatter.43
  458.9 40.0 reduce-scatter.45
  501.4 40.1 reduce-scatter.47
  562.7 39.9 reduce-scatter.49
  605.2 40.2 reduce-scatter.51
  666.4 39.9 reduce-scatter.53
  708.9 40.2 reduce-scatter.55
  752.2 43.3 all-reduce.4
  798.5 321.7 reduce-scatter.37
  1123.4 315.6 reduce-scatter.39
  1442.1 317.7 reduce-scatter.59
  1763.0 318.0 reduce-scatter.57
where the time goes:
time: 2100 us; the launch traced here: 2090 us
  waiting for transfers between devices  1470 us (70%)
  blocking collectives  399 us (19%)
  matrix products  101 us (5%)
  local copies, waits for them, and re-layouts  69.9 us (3%)
    unnamed x23, waiting for transfers between devices  929 us
    reduce_scatter x1, waiting for transfers between devices, shards(): lax.psum_scatter(grad_key_w[None], ('dp', 'seq'), scatter_dimension=1, ti...  319 us
    reduce_scatter x1, waiting for transfers between devices, shards(): lax.psum_scatter(grad_query_w[None], ('dp', 'seq'), scatter_dimension=1,...  188 us
    unnamed x1, blocking collectives  158 us
    all_gather x4, blocking collectives, forward_layer(): lax.all_gather(value_local, 'seq', axis=0, tiled=True)  121 us
    all_gather x4, blocking collectives, forward_layer(): lax.all_gather(key_local, 'seq', axis=0, tiled=True)  120 us
  transfers between devices with their start and end apart: 19, of which 18 were waited for; matrix products, arithmetic and copies ran while one was open for 3% of the time, Pallas kernels for 0%

commit v1 on v0

--- a/solution.py
+++ b/solution.py
@@ -7,6 +7,13 @@
 KEY = 64
 VALUE = 96
 epsilon = 1e-05
+
+
+def exchange_gather(x, mesh_axis, dim):
+    size = lax.axis_size(mesh_axis)
+    shards = jnp.stack([x for _ in range(size)])
+    shards = lax.all_to_all(shards, mesh_axis, split_axis=0, concat_axis=0)
+    return jnp.concatenate(shards, axis=dim)
 
 
 def passed_along(block, axis, distance):
@@ -66,7 +73,7 @@
     )
     key_all, value_all = (
         lax.all_gather(key_local, "seq", axis=0, tiled=True),
-        lax.all_gather(value_local, "seq", axis=0, tiled=True),
+        exchange_gather(value_local, "seq", 0),
     )
     expo = exp_scores_of(query_local, key_all)
     totals = jnp.sum(expo, axis=-1)

time: 2100 us -> 2030 us (0.967)
  blocking collectives: 399 us -> 291 us
    all_gather x4 -> x0, blocking collectives: 121 us -> none  [forward_layer(): lax.all_gather(value_local, 'seq', axis=0, tiled=True)]
  transfers between devices with their start and end apart: 19 -> 23, of which waited for: 18 -> 18; matrix products, arithmetic and copies ran while one was open for 3% -> 5% of each run, Pallas kernels for 0% -> 0%
where the time goes in v1:
time: 2030 us; the launch traced here: 2020 us
  waiting for transfers between devices  1470 us (72%)
  blocking collectives  291 us (14%)
  matrix products  115 us (6%)
  local copies, waits for them, and re-layouts  82.3 us (4%)
  starting transfers between devices  30.2 us (1%)
    unnamed x23, waiting for transfers between devices  928 us
    reduce_scatter x1, waiting for transfers between devices, shards(): lax.psum_scatter(grad_key_w[None], ('dp', 'seq'), scatter_dimension=1, ti...  318 us
    reduce_scatter x1, waiting for transfers between devices, shards(): lax.psum_scatter(grad_query_w[None], ('dp', 'seq'), scatter_dimension=1,...  188 us
    unnamed x1, blocking collectives  158 us
    all_gather x4, blocking collectives, forward_layer(): lax.all_gather(key_local, 'seq', axis=0, tiled=True)  132 us
  transfers between devices with their start and end apart: 23, of which 18 were waited for; matrix products, arithmetic and copies ran while one was open for 5% of the time, Pallas kernels for 0%

profile of v1, /device:TPU:16, one launch (start us, length us, event | category | flops | bytes accessed | tf_op | source)
XLA Modules:
  0.0 2023.6 jit_solution(524153620109669000)
XLA Ops:
  13.1 5.0 all-to-all-start
  19.6 34.4 %all_gather.12 = bf16[1024,256]{1,0:T(8,128)(2,1)S(1)} all-gather(bf16[128,256]{1,0:T(8,128)(2,1)S(1)} %convolution_convert_fusion.14), channel_id=1, replica_groups=mesh['dp'=8,'section'=4,'seq'=8] {'seq'}, dimensions={0}, use_global_device_ids=true | all-gather | bytes 589824 | tf_op jit(solution)/shard_map/all_gather | solution.py:75
  65.7 8.7 collective-permute-done
  88.9 33.6 %all_gather.13 = bf16[1024,256]{1,0:T(8,128)(2,1)} all-gather(bf16[128,256]{1,0:T(8,128)(2,1)S(1)} %convolution_convert_fusion.12), channel_id=1, replica_groups=mesh['dp'=8,'section'=4,'seq'=8] {'seq'}, dimensions={0}, use_global_device_ids=true | all-gather | bytes 589824 | tf_op jit(solution)/shard_map/all_gather | solution.py:75
  137.1 8.7 collective-permute-done.1
  160.4 33.7 %all_gather.14 = bf16[1024,256]{1,0:T(8,128)(2,1)} all-gather(bf16[128,256]{1,0:T(8,128)(2,1)S(1)} %convolution_convert_fusion.10), channel_id=1, replica_groups=mesh['dp'=8,'section'=4,'seq'=8] {'seq'}, dimensions={0}, use_global_device_ids=true | all-gather | bytes 589824 | tf_op jit(solution)/shard_map/all_gather | solution.py:75
  213.1 5.1 collective-permute-done.2
  226.0 30.7 %all_gather.15 = bf16[1024,256]{1,0:T(8,128)(2,1)S(1)} all-gather(bf16[128,256]{1,0:T(8,128)(2,1)S(1)} %convolution_convert_fusion.9), channel_id=1, replica_groups=mesh['dp'=8,'section'=4,'seq'=8] {'seq'}, dimensions={0}, use_global_device_ids=true | all-gather | bytes 589824 | tf_op jit(solution)/shard_map/all_gather | solution.py:75
  294.6 35.3 %reduce-scatter.42.cloned.1.call-done = bf16[128,256]{1,0:T(8,128)(2,1)} async-done(((bf16[1024,256]{1,0:T(8,128)(2,1)}), bf16[128,256]{1,0:T(8,128)(2,1)}) %reduce-scatter.42.cloned.1.call-update) | async-done | bytes 65552
  332.3 40.2 %reduce-scatter.44.cloned.1.call-done = bf16[128,384]{1,0:T(8,128)(2,1)} async-done(((bf16[1024,384]{1,0:T(8,128)(2,1)}), bf16[128,384]{1,0:T(8,128)(2,1)}) %reduce-scatter.44.cloned.1.call-update) | async-done | bytes 98320
  378.0 5.1 collective-permute-done.3
  403.1 31.4 %reduce-scatter.46.cloned.1.call-done = bf16[128,256]{1,0:T(8,128)(2,1)} async-done(((bf16[1024,256]{1,0:T(8,128)(2,1)}), bf16[128,256]{1,0:T(8,128)(2,1)}) %reduce-scatter.46.cloned.1.call-update) | async-done | bytes 65552
  437.2 39.9 %reduce-scatter.48.cloned.1.call-done = bf16[128,384]{1,0:T(8,128)(2,1)} async-done(((bf16[1024,384]{1,0:T(8,128)(2,1)}), bf16[128,384]{1,0:T(8,128)(2,1)}) %reduce-scatter.48.cloned.1.call-update) | async-done | bytes 98320
  481.8 5.3 collective-permute-done.4
  507.1 31.4 %reduce-scatter.50.cloned.1.call-done = bf16[128,256]{1,0:T(8,128)(2,1)} async-done(((bf16[1024,256]{1,0:T(8,128)(2,1)}), bf16[128,256]{1,0:T(8,128)(2,1)}) %reduce-scatter.50.cloned.1.call-update) | async-done | bytes 65552
  541.2 39.9 %reduce-scatter.52.cloned.1.call-done = bf16[128,384]{1,0:T(8,128)(2,1)} async-done(((bf16[1024,384]{1,0:T(8,128)(2,1)}), bf16[128,384]{1,0:T(8,128)(2,1)}) %reduce-scatter.52.cloned.1.call-update) | async-done | bytes 98320
  585.7 5.3 collective-permute-done.5
  614.9 27.2 %reduce-scatter.54.cloned.1.call-done = bf16[128,256]{1,0:T(8,128)(2,1)} async-done(((bf16[1024,256]{1,0:T(8,128)(2,1)}), bf16[128,256]{1,0:T(8,128)(2,1)}) %reduce-scatter.54.cloned.1.call-update) | async-done | bytes 65552
  644.6 40.2 %reduce-scatter.56.cloned.1.call-done = bf16[128,384]{1,0:T(8,128)(2,1)} async-done(((bf16[1024,384]{1,0:T(8,128)(2,1)}), bf16[128,384]{1,0:T(8,128)(2,1)}) %reduce-scatter.56.cloned.1.call-update) | async-done | bytes 98320
  707.5 158.1 %all-reduce = f32[1,1536]{1,0:T(1,128)S(1)} all-reduce(f32[1,1536]{1,0:T(1,128)S(1)} %select_n.365), channel_id=10, replica_groups=mesh['dp'=8,'section'=4,'seq'=8] {'dp','seq'}, use_global_device_ids=true, to_apply=%region_37.38.clone | all-reduce | flops 1536 | bytes 12288
  867.8 188.3 %reduce-scatter.38.cloned.1.call-done = f32[1,24,256]{2,1,0:T(8,128)} async-done(((f32[1,1536,256]{2,1,0:T(8,128)}), f32[1,24,256]{2,1,0:T(8,128)}) %reduce-scatter.38.cloned.1.call-update) | async-done | bytes 24592 | tf_op jit(solution)/shard_map/reduce_scatter | solution.py:226
  1056.0 318.5 %reduce-scatter.40.cloned.1.call-done = f32[1,24,256]{2,1,0:T(8,128)} async-done(((f32[1,1536,256]{2,1,0:T(8,128)}), f32[1,24,256]{2,1,0:T(8,128)}) %reduce-scatter.40.cloned.1.call-update) | async-done | bytes 24592 | tf_op jit(solution)/shard_map/reduce_scatter | solution.py:227
  1374.5 321.0 %reduce-scatter.60.cloned.1.call-done = f32[1,24,384]{2,1,0:T(8,128)} async-done(((f32[1,1536,384]{2,1,0:T(8,128)}), f32[1,24,384]{2,1,0:T(8,128)}) %reduce-scatter.60.cloned.1.call-update) | async-done | bytes 36880
  1695.5 321.4 %reduce-scatter.58.cloned.1.call-done = f32[1,24,384]{2,1,0:T(8,128)} async-done(((f32[1,1536,384]{2,1,0:T(8,128)}), f32[1,24,384]{2,1,0:T(8,128)}) %reduce-scatter.58.cloned.1.call-update) | async-done | bytes 36880
  (411 shorter events, 239.1 us)
Async XLA Ops:
  13.1 42.9 %all-to-all-start = ((bf16[8,128,384]{1,2,0:T(8,128)(2,1)}), bf16[8,128,384]{1,2,0:T(8,128)(2,1)}, u32[]{:S(2)}, u32[]{:S(2)}) async-start(bf16[8,128,384]{1,2,0:T(8,128)(2,1)} %stack.8), calls=%async_computation | async-start | bytes 1572864 | tf_op jit(solution)/shard_map/all_to_all | solution.py:15
  63.7 10.6 collective-permute-start
  83.2 44.3 %all-to-all-start.1 = ((bf16[8,128,384]{1,2,0:T(8,128)(2,1)}), bf16[8,128,384]{1,2,0:T(8,128)(2,1)}, u32[]{:S(2)}, u32[]{:S(2)}) async-start(bf16[8,128,384]{1,2,0:T(8,128)(2,1)} %stack.9), calls=%async_computation.1 | async-start | bytes 1572864 | tf_op jit(solution)/shard_map/all_to_all | solution.py:15
  135.1 10.6 collective-permute-start.1
  154.7 44.3 %all-to-all-start.2 = ((bf16[8,128,384]{1,2,0:T(8,128)(2,1)}), bf16[8,128,384]{1,2,0:T(8,128)(2,1)}, u32[]{:S(2)}, u32[]{:S(2)}) async-start(bf16[8,128,384]{1,2,0:T(8,128)(2,1)} %stack.10), calls=%async_computation.2 | async-start | bytes 1572864 | tf_op jit(solution)/shard_map/all_to_all | solution.py:15
  207.4 10.8 collective-permute-start.2
  258.8 14.7 all-to-all-start.3
  263.1 66.7 %reduce-scatter.42.cloned.1.call-start = ((), (), s32[]{:S(2)}) async-start(), calls=%async_computation.19 | async-start | bytes 589824
  286.2 86.4 %reduce-scatter.44.cloned.1.call-start = ((), (), s32[]{:S(2)}) async-start(), calls=%async_computation.20 | async-start | bytes 884736
  290.8 143.8 %reduce-scatter.46.cloned.1.call-start = ((), (), s32[]{:S(2)}) async-start(), calls=%async_computation.21 | async-start | bytes 589824
  292.7 79.9 %copy-start.22 = (bf16[1,128,1536]{2,1,0:T(8,128)(2,1)S(1)}, bf16[1,128,1536]{2,1,0:T(8,128)(2,1)}, u32[]{:S(2)}) copy-start(bf16[1,128,1536]{2,1,0:T(8,128)(2,1)} %param.7) | copy-start | bytes 1179652
  375.9 7.2 collective-permute-start.3
  394.3 82.8 %reduce-scatter.48.cloned.1.call-start = ((), (), s32[]{:S(2)}) async-start(), calls=%async_computation.22 | async-start | bytes 884736
  399.2 139.3 %reduce-scatter.50.cloned.1.call-start = ((), (), s32[]{:S(2)}) async-start(), calls=%async_computation.23 | async-start | bytes 589824
  479.9 7.2 collective-permute-start.4
  498.3 82.8 %reduce-scatter.52.cloned.1.call-start = ((), (), s32[]{:S(2)}) async-start(), calls=%async_computation.24 | async-start | bytes 884736
  503.2 139.0 %reduce-scatter.54.cloned.1.call-start = ((), (), s32[]{:S(2)}) async-start(), calls=%async_computation.25 | async-start | bytes 589824
  583.8 7.2 collective-permute-start.5
  602.0 82.9 %reduce-scatter.56.cloned.1.call-start = ((), (), s32[]{:S(2)}) async-start(), calls=%async_computation.26 | async-start | bytes 884736
  606.6 259.6 %all-reduce.5.cloned.1.call-start = ((), (), s32[]{:S(2)}) async-start(), calls=%async_computation.16 | async-start | bytes 786432 | tf_op jit(solution)/shard_map/psum | solution.py:27
  687.8 368.3 %reduce-scatter.38.cloned.1.call-start = ((), (), s32[]{:S(2)}) async-start(), calls=%async_computation.17 | async-start | bytes 1597440 | tf_op jit(solution)/shard_map/reduce_scatter | solution.py:226
  692.2 682.3 %reduce-scatter.40.cloned.1.call-start = ((), (), s32[]{:S(2)}) async-start(), calls=%async_computation.18 | async-start | bytes 1597440 | tf_op jit(solution)/shard_map/reduce_scatter | solution.py:227
  695.5 1000.0 %reduce-scatter.60.cloned.1.call-start = ((), (), s32[]{:S(2)}) async-start(), calls=%async_computation.28 | async-start | bytes 2396160
  700.4 1316.4 %reduce-scatter.58.cloned.1.call-start = ((), (), s32[]{:S(2)}) async-start(), calls=%async_computation.27 | async-start | bytes 2396160
  (107 other events, 669.6 us)
Sparse Core Ops, SparseCore 0:
  286.3 43.4 reduce-scatter.41
  332.4 40.1 reduce-scatter.43
  394.4 40.0 reduce-scatter.45
  437.0 40.1 reduce-scatter.47
  498.4 40.0 reduce-scatter.49
  540.9 40.1 reduce-scatter.51
  602.1 39.9 reduce-scatter.53
  644.7 40.1 reduce-scatter.55
  687.9 43.3 all-reduce.4
  734.2 321.7 reduce-scatter.37
  1059.1 315.3 reduce-scatter.39
  1377.4 318.0 reduce-scatter.59
  1698.6 318.2 reduce-scatter.57
